TPU v7x, 128 devices: a whole 4x4x4 slice. The times are simulated.
128 devices in a mesh: walker: 32 (over x, z, core), owner: 4 (over y).
Axes of the slice: x: 4, y: 4, z: 4, core: 2. Of those that a mesh axis runs over, the one named last changes fastest.
Arguments:
- block_input_rows: bfloat16 [2048, 1024, 256], P(('walker', 'owner')), may hold values from -6 to 6
- spin_values: int32 [2048, 1024], P(('walker', 'owner')), may hold values 0 or 1
- conv_weight: bfloat16 [256, 512], replicated, may hold values from -0.25 to 0.25
- conv_bias: float32 [256], replicated, may hold values from -3 to 3
- readout: float32 [256], replicated, may hold values from -0.375 to 0.375
- energies: float32 [2048], P(('walker', 'owner')), may hold values from -1 to 0.1
- basis_out: bfloat16 [256, 256], P(None, 'owner'), may hold values from -0.375 to 0.375
- basis_in: bfloat16 [512, 512], P(None, 'owner'), may hold values from -6 to 6
Outputs:
- moment_stats: float32 [256, 512], P(None, 'owner')
- update: float32 [256, 512], P(None, 'owner')
All inputs are finite; a program needn't handle non-finite values. No bound on the sum of `spin_values` on one device may be relied on, other than what follows from the above.
Results may differ from a plain program's by a relative error of at most 0.025.
Values may be sent and summed in bfloat16 or wider, within the bound.
A program may use at most 128 MiB of HBM per device.

v0:
```python
import jax
import jax.numpy as jnp
from jax import lax
from jax.sharding import PartitionSpec as P

DILATION_STEP = 16
DAMPING = 0.01


def body(
    block_input_rows, spin_values, conv_weight, conv_bias, readout, energies, basis_out, basis_in
):
    local_sample_count = block_input_rows.shape[0]
    chain_site_count = block_input_rows.shape[1]
    channel_count = block_input_rows.shape[2]
    total_samples = local_sample_count * lax.axis_size("walker") * lax.axis_size("owner")
    energy_total = lax.psum(jnp.sum(energies), ("walker", "owner"))
    energy_mean = energy_total / total_samples
    full_out = lax.all_gather(basis_out, "owner", axis=1, tiled=True)
    now_part = jnp.einsum(
        "slc,oc->slo",
        block_input_rows,
        conv_weight[:, channel_count:],
        preferred_element_type=jnp.float32,
    )
    earlier_portion = jnp.einsum(
        "slc,oc->slo",
        block_input_rows,
        conv_weight[:, :channel_count],
        preferred_element_type=jnp.float32,
    )
    delayed_input = jnp.concatenate(
        [
            jnp.zeros((local_sample_count, DILATION_STEP, channel_count), jnp.float32),
            earlier_portion[:, : chain_site_count - DILATION_STEP],
        ],
        axis=1,
    )
    pre_act = now_part + delayed_input + conv_bias
    activation = jnp.tanh(pre_act)
    logit_rows = jnp.sum((block_input_rows.astype(jnp.float32) + activation) * readout, axis=-1)
    target = spin_values.astype(jnp.float32)
    backward_signal = (
        (0.5 * (target - jax.nn.sigmoid(logit_rows)))[:, :, None]
        * readout
        * (1.0 - activation * activation)
    )
    backward_signal = backward_signal.astype(jnp.bfloat16)
    grad_now = jnp.einsum(
        "slo,slc->soc", backward_signal, block_input_rows, preferred_element_type=jnp.float32
    )
    gradient_earlier = jnp.einsum(
        "slo,slc->soc",
        backward_signal[:, DILATION_STEP:],
        block_input_rows[:, : chain_site_count - DILATION_STEP],
        preferred_element_type=jnp.float32,
    )
    gradient = jnp.concatenate([gradient_earlier, grad_now], axis=2).astype(jnp.bfloat16)
    half_proj = jnp.einsum(
        "ok,soc->skc", full_out, gradient, preferred_element_type=jnp.float32
    ).astype(jnp.bfloat16)
    sample_weights = energies - energy_mean
    panel_width = basis_in.shape[1]
    projected = jnp.einsum(
        "skc,cm->skm",
        half_proj,
        lax.all_gather(basis_in, "owner", axis=1, tiled=True),
        preferred_element_type=jnp.float32,
    )
    squares = jnp.sum(projected * projected, axis=0)
    weighted = jnp.einsum("s,skm->km", sample_weights, projected)
    stacked = jnp.stack([squares, weighted], axis=0)
    totals = lax.psum(stacked, ("walker", "owner"))
    owner_panel = lax.dynamic_slice_in_dim(
        totals, lax.axis_index("owner") * panel_width, panel_width, 2
    )
    stats_part = owner_panel[0] / total_samples
    centered = owner_panel[1] / total_samples
    ratio_float = centered / (stats_part + DAMPING)
    scaled_ratio = ratio_float.astype(jnp.bfloat16)
    mixed_basis = jnp.dot(full_out, scaled_ratio, preferred_element_type=jnp.float32).astype(
        jnp.bfloat16
    )
    back_term = jnp.dot(mixed_basis, basis_in.T, preferred_element_type=jnp.float32)
    raw_update = lax.psum_scatter(back_term, "owner", scatter_dimension=1, tiled=True)
    square_total = lax.psum(jnp.sum(raw_update * raw_update), "owner")
    mean_sq = square_total / (channel_count * 2 * channel_count)
    return (stats_part, raw_update / jnp.sqrt(mean_sq + 1e-06))


def solution(mesh):
    in_specs = (
        P(("walker", "owner"), None, None),
        P(("walker", "owner"), None),
        P(),
        P(),
        P(),
        P(("walker", "owner")),
        P(None, "owner"),
        P(None, "owner"),
    )
    out_specs = (P(None, "owner"), P(None, "owner"))
    return jax.shard_map(body, mesh=mesh, in_specs=in_specs, out_specs=out_specs, check_vma=False)
```

profile of v0, /device:TPU:0, one launch (start us, length us, event | category | flops | bytes accessed | tf_op | source)
XLA Modules:
  0.0 357.1 jit_solution(8199990316887416576)
XLA Ops:
  7.2 0.0 copy-start.2
  7.2 0.0 copy-start.6
  7.2 0.0 all-reduce.3.cloned.1.call-start
  7.2 11.4 %fusion.5 = f32[16,1008,256]{2,1,0:T(8,128)} fusion(bf16[16,1024,256]{2,1,0:T(8,128)(2,1)} %param.8, bf16[256,512]{1,0:T(8,128)(2,1)} %param.10), kind=kOutput, calls=%fused_computation.9 | convolution fusion | flops 2113929216 | bytes 24903680 | tf_op jit(solution)/shard_map/slc,oc->slo/dot_general | solution.py:26
  18.6 0.0 copy-done.6
  18.6 0.0 copy-start.3
  18.6 16.8 %multiply_reduce_fusion = (f32[16,1024]{1,0:T(8,128)S(1)}, f32[16,1024,256]{2,1,0:T(8,128)}) fusion(bf16[16,1024,256]{2,1,0:T(8,128)(2,1)} %param.8, f32[256]{0:T(256)S(1)} %copy-done.5, f32[256]{0:T(256)S(1)} %copy-done.6, f32[16,1008,256]{2,1,0:T(8,128)} %fusion.5, bf16[256,512]{1,0:T(8,128)(2,1)S(1)} %copy-done.2), kind=kOutput, calls=%fused_computation.1 | convolution fusion | flops 2172633088 | bytes 50268160 | tf_op jit(solution)/shard_map/slc,oc->slo/dot_general | solution.py:20
  35.5 10.0 %multiply_convert_fusion = bf16[16,1024,256]{2,1,0:T(8,128)(2,1)} fusion(f32[16,1024,256]{2,1,0:T(8,128)} %get-tuple-element.3, f32[16,1024]{1,0:T(8,128)S(1)} %subtract_multiply_fusion, f32[256]{0:T(256)S(1)} %copy-done.5), kind=kLoop, calls=%fused_computation | loop fusion | flops 20971520 | bytes 25232384 | tf_op jit(solution)/shard_map/convert_element_type | solution.py:48
  45.5 8.2 %convolution_convert_fusion = bf16[16,256,256]{2,1,0:T(8,128)(2,1)S(1)} fusion(bf16[16,1024,256]{2,1,0:T(8,128)(2,1)} %multiply_convert_fusion, bf16[16,1024,256]{2,1,0:T(8,128)(2,1)} %param.8), kind=kOutput, calls=%fused_computation.19 | convolution fusion | flops 2148532224 | bytes 18874368 | tf_op jit(solution)/shard_map/slo,slc->soc/dot_general | solution.py:49
  53.8 0.0 copy-start
  53.8 0.0 copy-start.7
  53.8 0.0 copy-start.4
  53.8 9.6 %fusion.18 = bf16[16,256,256]{2,1,0:T(8,128)(2,1)} fusion(bf16[16,1024,256]{2,1,0:T(8,128)(2,1)} %param.8, bf16[16,1024,256]{2,1,0:T(8,128)(2,1)} %multiply_convert_fusion), kind=kOutput, calls=%fused_computation.18 | convolution fusion | flops 2114977792 | bytes 18612224 | tf_op jit(solution)/shard_map/slo,slc->soc/dot_general | solution.py:52
  63.4 14.6 %all_gather.7 = bf16[512,512]{1,0:T(8,128)(2,1)S(1)} all-gather(bf16[512,128]{1,0:T(8,128)(2,1)S(1)} %copy-done), channel_id=1, replica_groups=mesh['walker'=32,'owner'=4] {'owner'}, dimensions={1}, use_global_device_ids=true | all-gather | bytes 655360 | tf_op jit(solution)/shard_map/all_gather | solution.py:67
  78.1 0.6 reduce_sum.38
  78.7 0.0 copy-done.4
  78.7 12.0 %all_gather.6 = bf16[256,256]{0,1:T(8,128)(2,1)S(1)} all-gather(bf16[256,64]{0,1:T(8,128)(2,1)S(1)} %copy-done.4), channel_id=1, replica_groups=mesh['walker'=32,'owner'=4] {'owner'}, dimensions={1}, use_global_device_ids=true | all-gather | bytes 163840 | tf_op jit(solution)/shard_map/all_gather | solution.py:19
  90.6 66.1 %psum.21 = f32[]{:T(128)} all-reduce(f32[]{:T(128)} %reduce_sum.38), channel_id=1, replica_groups=mesh['walker'=32,'owner'=4] {'walker','owner'}, use_global_device_ids=true, to_apply=%region_3.0 | all-reduce | flops 1 | bytes 8 | tf_op jit(solution)/shard_map/psum | solution.py:17
  157.4 6.2 %multiply_reduce_fusion.1 = (f32[256,512]{1,0:T(8,128)S(1)}, bf16[16,256,512]{2,1,0:T(8,128)(2,1)}) fusion(bf16[512,512]{1,0:T(8,128)(2,1)S(1)} %all_gather.7, bf16[16,256,256]{2,1,0:T(8,128)(2,1)S(1)} %convolution_convert_fusion, bf16[16,256,256]{2,1,0:T(8,128)(2,1)} %fusion.18, bf16[256,256]{0,1:T(8,128)(2,1)S(1)} %all_gather.6), kind=kOutput, calls=%fused_computation.5 | convolution fusion | flops 3237871616 | bytes 9568256 | tf_op jit(solution)/shard_map/skc,cm->skm/dot_general | solution.py:64
  163.6 4.7 %fusion = f32[1,256,512]{2,0,1:T(1,128)S(1)} fusion(bf16[16,256,512]{2,1,0:T(8,128)(2,1)} %get-tuple-element.5, f32[16]{0:T(128)S(1)} %copy-done.7, f32[]{:T(128)S(6)} %div.29), kind=kOutput, calls=%fused_computation.3 | convolution fusion | flops 4194320 | bytes 4718660 | tf_op jit(solution)/shard_map/s,skm->km/dot_general | solution.py:71
  168.4 1.1 pad_maximum_fusion
  169.5 0.0 all-reduce.3.cloned.1.call-update
  169.5 0.0 reduce-scatter.2.cloned.1.call-start
  169.5 144.0 %all-reduce.3.cloned.1.call-done = f32[2,256,512]{2,1,0:T(8,128)} async-done(((f32[2,256,512]{2,1,0:T(8,128)}), f32[2,256,512]{2,1,0:T(8,128)}) %all-reduce.3.cloned.1.call-update) | async-done | bytes 1048592 | tf_op jit(solution)/shard_map/psum | solution.py:73
  313.5 0.9 fusion.28
  314.4 0.0 copy-start.1
  314.4 2.2 fusion.23
  316.7 0.0 reduce-scatter.2.cloned.1.call-update
  316.7 20.8 %reduce-scatter.2.cloned.1.call-done = f32[256,128]{1,0:T(8,128)} async-done(((f32[256,512]{1,0:T(8,128)}), f32[256,128]{1,0:T(8,128)}) %reduce-scatter.2.cloned.1.call-update) | async-done | bytes 131088 | tf_op jit(solution)/shard_map/reduce_scatter | solution.py:85
  337.5 1.5 multiply_reduce_fusion.2
  339.0 9.0 %psum.23 = f32[]{:T(128)} all-reduce(f32[]{:T(128)} %multiply_reduce_fusion.2), channel_id=1, replica_groups=mesh['walker'=32,'owner'=4] {'owner'}, use_global_device_ids=true, to_apply=%region_7.0 | all-reduce | flops 1 | bytes 8 | tf_op jit(solution)/shard_map/psum | solution.py:86
  348.7 1.6 broadcast_divide_fusion
  (9 shorter events, 0.1 us)
Async XLA Ops:
  7.2 11.5 %copy-start.2 = (bf16[256,512]{1,0:T(8,128)(2,1)S(1)}, bf16[256,512]{1,0:T(8,128)(2,1)}, u32[]{:S(2)}) copy-start(bf16[256,512]{1,0:T(8,128)(2,1)} %param.10) | copy-start | bytes 786436
  7.2 11.5 %copy-start.6 = (f32[256]{0:T(256)S(1)}, f32[256]{0:T(256)}, u32[]{:S(2)}) copy-start(f32[256]{0:T(256)} %param.11) | copy-start | bytes 3076
  7.2 11.4 %copy-start.5 = (f32[256]{0:T(256)S(1)}, f32[256]{0:T(256)}, u32[]{:S(2)}) copy-start(f32[256]{0:T(256)} %param.12) | copy-start | bytes 3076
  7.2 306.3 %all-reduce.3.cloned.1.call-start = ((), (), s32[]{:S(2)}) async-start(), calls=%async_computation.1 | async-start | bytes 2097152 | tf_op jit(solution)/shard_map/psum | solution.py:73
  18.6 16.8 %copy-start.3 = (s32[16,1024]{1,0:T(8,128)S(1)}, s32[16,1024]{1,0:T(8,128)}, u32[]{:S(2)}) copy-start(s32[16,1024]{1,0:T(8,128)} %param.9) | copy-start | bytes 196612
  53.8 9.6 %copy-start = (bf16[512,128]{1,0:T(8,128)(2,1)S(1)}, bf16[512,128]{1,0:T(8,128)(2,1)}, u32[]{:S(2)}) copy-start(bf16[512,128]{1,0:T(8,128)(2,1)} %param.15) | copy-start | bytes 393220
  53.8 24.3 %copy-start.7 = (f32[16]{0:T(128)S(1)}, f32[16]{0:T(128)}, u32[]{:S(2)}) copy-start(f32[16]{0:T(128)} %param.13) | copy-start | bytes 196
  53.8 24.9 %copy-start.4 = (bf16[256,64]{0,1:T(8,128)(2,1)S(1)}, bf16[256,64]{0,1:T(8,128)(2,1)}, u32[]{:S(2)}) copy-start(bf16[256,64]{0,1:T(8,128)(2,1)} %param.14) | copy-start | bytes 98308
  169.5 168.0 %reduce-scatter.2.cloned.1.call-start = ((), (), s32[]{:S(2)}) async-start(), calls=%async_computation.2 | async-start | bytes 655360 | tf_op jit(solution)/shard_map/reduce_scatter | solution.py:85
  314.4 35.9 %copy-start.1 = (f32[256,128]{1,0:T(8,128)}, f32[256,128]{1,0:T(8,128)S(1)}, u32[]{:S(2)}) copy-start(f32[256,128]{1,0:T(8,128)S(1)} %fusion.28) | copy-start | bytes 393220
Sparse Core Ops, SparseCore 0:
  169.6 143.8 all-reduce.2
  316.8 20.6 reduce-scatter.1
where the time goes:
time: 358 us; the launch traced here: 357 us
  waiting for transfers between devices  165 us (46%)
  blocking collectives  102 us (28%)
  matrix products  59.2 us (17%)
  other arithmetic  15.8 us (4%)
  between operations  15.5 us (4%)
    psum x1, waiting for transfers between devices, body(): totals = lax.psum(stacked, ('walker', 'owner'))  144 us
    psum x1, blocking collectives, body(): energy_total = lax.psum(jnp.sum(energies), ('walker', 'owner'))  66.1 us
    reduce_scatter x1, waiting for transfers between devices, body(): lax.psum_scatter(back_term, 'owner', scatter_dimension=1, tiled=True)  20.8 us
    dot_general x1, matrix products, body(): jnp.einsum('slc,oc->slo', block_input_rows, conv_weight[:, channel_count:...  16.8 us
    all_gather x1, blocking collectives, body(): lax.all_gather(basis_in, 'owner', axis=1, tiled=True)  14.6 us
    all_gather x1, blocking collectives, body(): full_out = lax.all_gather(basis_out, 'owner', axis=1, tiled=True)  12 us
    dot_general x1, matrix products, body(): jnp.einsum('slc,oc->slo', block_input_rows, conv_weight[:, :channel_count...  11.4 us
    convert_element_type x1, other arithmetic, body(): backward_signal = backward_signal.astype(jnp.bfloat16)  10 us
  transfers between devices with their start and end apart: 2, of which 2 were waited for; matrix products, arithmetic and copies ran while one was open for 0% of the time, Pallas kernels for 0%

commit v1 on v0

--- a/solution.py
+++ b/solution.py
@@ -5,6 +5,12 @@
 
 DILATION_STEP = 16
 DAMPING = 0.01
+
+
+def in_order(tiles, dim):
+    tiles = jnp.moveaxis(tiles, 0, dim)
+    lengths = tiles.shape
+    return tiles.reshape(*lengths[:dim], lengths[dim] * lengths[dim + 1], *lengths[dim + 2 :])
 
 
 def body(
@@ -16,7 +22,19 @@
     total_samples = local_sample_count * lax.axis_size("walker") * lax.axis_size("owner")
     energy_total = lax.psum(jnp.sum(energies), ("walker", "owner"))
     energy_mean = energy_total / total_samples
-    full_out = lax.all_gather(basis_out, "owner", axis=1, tiled=True)
+    count = lax.axis_size("owner")
+    pairs = [(i, (i + 1) % count) for i in range(count)]
+    back = [(b, a) for a, b in pairs]
+    lower, upper = ([], [])
+    for lap in range(count - 1):
+        if lap % 2 == 0:
+            lower.append(lax.ppermute(lower[-1] if lower else basis_out, "owner", pairs))
+        else:
+            upper.append(lax.ppermute(upper[-1] if upper else basis_out, "owner", back))
+    blocks = jnp.stack([*lower[::-1], basis_out, *upper])
+    shift = lax.axis_index("owner") - len(lower)
+    blocks = blocks[(jnp.arange(count) - shift) % count]
+    full_out = in_order(blocks, 1)
     now_part = jnp.einsum(
         "slc,oc->slo",
         block_input_rows,

time: 358 us -> 350 us (0.978)
  blocking collectives: 102 us -> 87.9 us
  starting transfers between devices: 0.08 us -> 4.84 us
    all_gather x1 -> x0, blocking collectives: 12 us -> none  [body(): full_out = lax.all_gather(basis_out, 'owner', axis=1, tiled=True)]
    ppermute x0 -> x3, starting transfers between devices: none -> 4.76 us  [the longest x2 3.18 us: body(): lax.ppermute(lower[-1] if lower else basis_out, 'owner', pairs)]
  transfers between devices with their start and end apart: 2 -> 5, of which waited for: 2 -> 2; matrix products, arithmetic and copies ran while one was open for 0% -> 16% of each run, Pallas kernels for 0% -> 0%
where the time goes in v1:
time: 350 us; the launch traced here: 349 us
  waiting for transfers between devices  165 us (47%)
  blocking collectives  87.9 us (25%)
  matrix products  59.1 us (17%)
  other arithmetic  16.5 us (5%)
  between operations  15.5 us (4%)
  starting transfers between devices  4.84 us (1%)
    psum x1, waiting for transfers between devices, body(): totals = lax.psum(stacked, ('walker', 'owner'))  144 us
    psum x1, blocking collectives, body(): energy_total = lax.psum(jnp.sum(energies), ('walker', 'owner'))  65.6 us
    reduce_scatter x1, waiting for transfers between devices, body(): lax.psum_scatter(back_term, 'owner', scatter_dimension=1, tiled=True)  21 us
    dot_general x1, matrix products, body(): jnp.einsum('slc,oc->slo', block_input_rows, conv_weight[:, channel_count:...  16.8 us
    all_gather x1, blocking collectives, body(): lax.all_gather(basis_in, 'owner', axis=1, tiled=True)  13.4 us
    dot_general x1, matrix products, body(): jnp.einsum('slc,oc->slo', block_input_rows, conv_weight[:, :channel_count...  11.4 us
    convert_element_type x1, other arithmetic, body(): backward_signal = backward_signal.astype(jnp.bfloat16)  10 us
    dot_general x1, matrix products, body(): jnp.einsum('slo,slc->soc', backward_signal[:, DILATION_STEP:], block_inpu...  9.59 us
  transfers between devices with their start and end apart: 5, of which 2 were waited for; matrix products, arithmetic and copies ran while one was open for 16% of the time, Pallas kernels for 0%

profile of v1, /device:TPU:0, one launch (start us, length us, event | category | flops | bytes accessed | tf_op | source)
XLA Modules:
  0.0 349.4 jit_solution(11802975936836693615)
XLA Ops:
  7.2 0.0 all-reduce.3.cloned.1.call-start
  7.2 1.7 collective-permute-start
  8.9 1.6 collective-permute-start.2
  10.5 11.4 %fusion.5 = f32[16,1008,256]{2,1,0:T(8,128)} fusion(bf16[16,1024,256]{2,1,0:T(8,128)(2,1)} %param.8, bf16[256,512]{1,0:T(8,128)(2,1)} %param.10), kind=kOutput, calls=%fused_computation.10 | convolution fusion | flops 2113929216 | bytes 24903680 | tf_op jit(solution)/shard_map/slc,oc->slo/dot_general | solution.py:44
  21.9 0.0 copy-start.2
  21.9 16.8 %multiply_reduce_fusion = (f32[16,1024]{1,0:T(8,128)S(1)}, f32[16,1024,256]{2,1,0:T(8,128)}) fusion(bf16[16,1024,256]{2,1,0:T(8,128)(2,1)} %param.8, f32[256]{0:T(256)S(1)} %copy-done.4, f32[256]{0:T(256)S(1)} %copy-done.5, f32[16,1008,256]{2,1,0:T(8,128)} %fusion.5, bf16[256,512]{1,0:T(8,128)(2,1)S(1)} %copy-done.1), kind=kOutput, calls=%fused_computation.2 | convolution fusion | flops 2172633088 | bytes 50268160 | tf_op jit(solution)/shard_map/slc,oc->slo/dot_general | solution.py:38
  38.8 10.0 %multiply_convert_fusion = bf16[16,1024,256]{2,1,0:T(8,128)(2,1)} fusion(f32[16,1024,256]{2,1,0:T(8,128)} %get-tuple-element.3, f32[16,1024]{1,0:T(8,128)S(1)} %subtract_multiply_fusion, f32[256]{0:T(256)S(1)} %copy-done.4), kind=kLoop, calls=%fused_computation.1 | loop fusion | flops 20971520 | bytes 25232384 | tf_op jit(solution)/shard_map/convert_element_type | solution.py:66
  48.8 8.2 %convolution_convert_fusion = bf16[16,256,256]{2,1,0:T(8,128)(2,1)S(1)} fusion(bf16[16,1024,256]{2,1,0:T(8,128)(2,1)} %multiply_convert_fusion, bf16[16,1024,256]{2,1,0:T(8,128)(2,1)} %param.8), kind=kOutput, calls=%fused_computation.20 | convolution fusion | flops 2148532224 | bytes 18874368 | tf_op jit(solution)/shard_map/slo,slc->soc/dot_general | solution.py:67
  57.1 0.0 copy-start
  57.1 0.0 copy-start.6
  57.1 0.0 copy-start.3
  57.1 9.6 %fusion.18 = bf16[16,256,256]{2,1,0:T(8,128)(2,1)} fusion(bf16[16,1024,256]{2,1,0:T(8,128)(2,1)} %param.8, bf16[16,1024,256]{2,1,0:T(8,128)(2,1)} %multiply_convert_fusion), kind=kOutput, calls=%fused_computation.19 | convolution fusion | flops 2114977792 | bytes 18612224 | tf_op jit(solution)/shard_map/slo,slc->soc/dot_general | solution.py:70
  66.7 13.4 %all_gather.3 = bf16[512,512]{1,0:T(8,128)(2,1)S(1)} all-gather(bf16[512,128]{1,0:T(8,128)(2,1)S(1)} %copy-done), channel_id=1, replica_groups=mesh['walker'=32,'owner'=4] {'owner'}, dimensions={1}, use_global_device_ids=true | all-gather | bytes 655360 | tf_op jit(solution)/shard_map/all_gather | solution.py:85
  80.1 0.6 reduce_sum.38
  80.7 0.0 collective-permute-done
  80.7 1.5 collective-permute-start.1
  82.2 65.6 %psum.21 = f32[]{:T(128)} all-reduce(f32[]{:T(128)} %reduce_sum.38), channel_id=1, replica_groups=mesh['walker'=32,'owner'=4] {'walker','owner'}, use_global_device_ids=true, to_apply=%region_3.4 | all-reduce | flops 1 | bytes 8 | tf_op jit(solution)/shard_map/psum | solution.py:23
  148.4 0.0 collective-permute-done.2
  148.4 0.6 gather_fusion
  149.0 6.2 %multiply_reduce_fusion.1 = (f32[256,512]{1,0:T(8,128)S(1)}, bf16[16,256,512]{2,1,0:T(8,128)(2,1)}) fusion(bf16[512,512]{1,0:T(8,128)(2,1)S(1)} %all_gather.3, bf16[256,256,1]{0,1,2:T(8,128)(2,1)S(1)} %bitcast.46, bf16[16,256,256]{2,1,0:T(8,128)(2,1)S(1)} %convolution_convert_fusion, bf16[16,256,256]{2,1,0:T(8,128)(2,1)} %fusion.18), kind=kOutput, calls=%fused_computation.6 | convolution fusion | flops 3237871616 | bytes 9568256 | tf_op jit(solution)/shard_map/skc,cm->skm/dot_general | solution.py:82
  155.2 4.7 %fusion = f32[1,256,512]{2,0,1:T(1,128)S(1)} fusion(bf16[16,256,512]{2,1,0:T(8,128)(2,1)} %get-tuple-element.5, f32[16]{0:T(128)S(1)} %copy-done.6, f32[]{:T(128)S(6)} %div.28), kind=kOutput, calls=%fused_computation.4 | convolution fusion | flops 4194320 | bytes 4718660 | tf_op jit(solution)/shard_map/s,skm->km/dot_general | solution.py:89
  160.0 1.1 pad_maximum_fusion
  161.1 0.0 all-reduce.3.cloned.1.call-update
  161.1 0.0 reduce-scatter.2.cloned.1.call-start
  161.1 143.9 %all-reduce.3.cloned.1.call-done = f32[2,256,512]{2,1,0:T(8,128)} async-done(((f32[2,256,512]{2,1,0:T(8,128)}), f32[2,256,512]{2,1,0:T(8,128)}) %all-reduce.3.cloned.1.call-update) | async-done | bytes 1048592 | tf_op jit(solution)/shard_map/psum | solution.py:91
  305.0 2.2 fusion.23
  307.2 0.0 reduce-scatter.2.cloned.1.call-update
  307.2 21.0 %reduce-scatter.2.cloned.1.call-done = f32[256,128]{1,0:T(8,128)} async-done(((f32[256,512]{1,0:T(8,128)}), f32[256,128]{1,0:T(8,128)}) %reduce-scatter.2.cloned.1.call-update) | async-done | bytes 131088 | tf_op jit(solution)/shard_map/reduce_scatter | solution.py:103
  328.3 1.5 multiply_reduce_fusion.2
  329.8 1.6 fusion.31
  331.4 8.9 %psum.23 = f32[]{:T(128)} all-reduce(f32[]{:T(128)} %multiply_reduce_fusion.2), channel_id=1, replica_groups=mesh['walker'=32,'owner'=4] {'owner'}, use_global_device_ids=true, to_apply=%region_7.8 | all-reduce | flops 1 | bytes 8 | tf_op jit(solution)/shard_map/psum | solution.py:104
  341.0 1.6 broadcast_divide_fusion
  (16 shorter events, 0.1 us)
Async XLA Ops:
  7.2 297.9 %all-reduce.3.cloned.1.call-start = ((), (), s32[]{:S(2)}) async-start(), calls=%async_computation.1 | async-start | bytes 2097152 | tf_op jit(solution)/shard_map/psum | solution.py:91
  7.2 73.5 %collective-permute-start = (bf16[256,64]{0,1:T(8,128)(2,1)}, bf16[256,64]{0,1:T(8,128)(2,1)S(1)}, u32[]{:S(2)}, u32[]{:S(2)}) collective-permute-start(bf16[256,64]{0,1:T(8,128)(2,1)} %param.14), channel_id=1, source_target_pairs={{0,1},{1,2},{2,3},{3,0},{4,5},{5,6},{6,7},{7,4},{8,9},{9,10},{10,1... | collective-permute-start | bytes 98312 | tf_op jit(solution)/shard_map/ppermute | solution.py:31
  8.9 139.4 %collective-permute-start.2 = (bf16[256,64]{0,1:T(8,128)(2,1)}, bf16[256,64]{0,1:T(8,128)(2,1)S(1)}, u32[]{:S(2)}, u32[]{:S(2)}) collective-permute-start(bf16[256,64]{0,1:T(8,128)(2,1)} %param.14), channel_id=1, source_target_pairs={{1,0},{2,1},{3,2},{0,3},{5,4},{6,5},{7,6},{4,7},{9,8},{10,9},{11,1... | collective-permute-start | bytes 98312 | tf_op jit(solution)/shard_map/ppermute | solution.py:33
  10.5 11.4 %copy-start.1 = (bf16[256,512]{1,0:T(8,128)(2,1)S(1)}, bf16[256,512]{1,0:T(8,128)(2,1)}, u32[]{:S(2)}) copy-start(bf16[256,512]{1,0:T(8,128)(2,1)} %param.10) | copy-start | bytes 786436
  10.5 11.4 %copy-start.4 = (f32[256]{0:T(256)S(1)}, f32[256]{0:T(256)}, u32[]{:S(2)}) copy-start(f32[256]{0:T(256)} %param.12) | copy-start | bytes 3076
  10.5 11.4 %copy-start.5 = (f32[256]{0:T(256)S(1)}, f32[256]{0:T(256)}, u32[]{:S(2)}) copy-start(f32[256]{0:T(256)} %param.11) | copy-start | bytes 3076
  21.9 16.8 %copy-start.2 = (s32[16,1024]{1,0:T(8,128)S(1)}, s32[16,1024]{1,0:T(8,128)}, u32[]{:S(2)}) copy-start(s32[16,1024]{1,0:T(8,128)} %param.9) | copy-start | bytes 196612
  57.1 9.6 %copy-start = (bf16[512,128]{1,0:T(8,128)(2,1)S(1)}, bf16[512,128]{1,0:T(8,128)(2,1)}, u32[]{:S(2)}) copy-start(bf16[512,128]{1,0:T(8,128)(2,1)} %param.15) | copy-start | bytes 393220
  57.1 23.0 %copy-start.6 = (f32[16]{0:T(128)S(1)}, f32[16]{0:T(128)}, u32[]{:S(2)}) copy-start(f32[16]{0:T(128)} %param.13) | copy-start | bytes 196
  57.1 91.3 %copy-start.3 = (bf16[256,64]{0,1:T(8,128)(2,1)S(1)}, bf16[256,64]{0,1:T(8,128)(2,1)}, u32[]{:S(2)}) copy-start(bf16[256,64]{0,1:T(8,128)(2,1)} %param.14) | copy-start | bytes 98308
  80.7 67.7 %collective-permute-start.1 = (bf16[256,64]{0,1:T(8,128)(2,1)S(1)}, bf16[256,64]{0,1:T(8,128)(2,1)S(1)}, u32[]{:S(2)}, u32[]{:S(2)}) collective-permute-start(bf16[256,64]{0,1:T(8,128)(2,1)S(1)} %collective-permute-done), channel_id=1, source_target_pairs={{0,1},{1,2},{2,3},{3,0},{4,5},{5,6},{6,7},{7,4},{8,9},{9,10},{10,1... | collective-permute-start | bytes 98312 | tf_op jit(solution)/shard_map/ppermute | solution.py:31
  161.1 167.2 %reduce-scatter.2.cloned.1.call-start = ((), (), s32[]{:S(2)}) async-start(), calls=%async_computation.2 | async-start | bytes 655360 | tf_op jit(solution)/shard_map/reduce_scatter | solution.py:103
Sparse Core Ops, SparseCore 0:
  161.2 143.7 all-reduce.2
  307.5 20.6 reduce-scatter.1
